TPU v7x, 32 devices: a whole 2x2x4 slice. The times are simulated.
32 devices in a mesh: grid: 4 (over z), elec: 8 (over y, x, core).
Axes of the slice: x: 2, y: 2, z: 4, core: 2. Of those that a mesh axis runs over, the one named last changes fastest.
Arguments:
- electric: bfloat16 [2, 8192, 8192], P(None, 'elec', 'grid'), may hold values from -6 to 6
- trial: bfloat16 [8192, 2, 128], P('grid'), may hold values from -0.0625 to 0.0625
- counts: int32 [8], replicated, may hold values from 1 to 1024, as said below
Outputs:
- field: float32 [8192, 2, 128], P(('grid', 'elec'))
Inputs may be any that keep to these rules, and one draw needn't show every extreme that they name: `counts`: at least one group holds exactly 1024 live electrons.
All inputs are finite; a program needn't handle non-finite values.
Results may differ from a plain program's by a relative error of at most 0.0023.
Values sent between devices are 32-bit elements; how exact they have to be, the bound alone decides.
A program may use at most 64 MiB of HBM per device.

v0:
```python
import jax
import jax.numpy as jnp
from jax import lax
from jax.sharding import PartitionSpec as P


def margin_block(electric_slab, trial_flat, mode_count):
    slab_count = electric_slab.shape[1]
    flattened = electric_slab.reshape(2 * slab_count, electric_slab.shape[2])
    products = jnp.dot(flattened, trial_flat, preferred_element_type=jnp.float32)
    real_part = products[:slab_count, :mode_count] + products[slab_count:, mode_count:]
    imag_part = products[:slab_count, mode_count:] - products[slab_count:, :mode_count]
    return jnp.stack([real_part, imag_part])


def field_block(electric_slab, coef_real, coef_imag):
    slab_count = electric_slab.shape[1]
    flattened = electric_slab.reshape(2 * slab_count, electric_slab.shape[2])
    coef_matrix = jnp.concatenate(
        [jnp.concatenate([coef_real, coef_imag], 1), jnp.concatenate([-coef_imag, coef_real], 1)], 0
    )
    return lax.dot_general(
        flattened, coef_matrix, (((0,), (0,)), ((), ())), preferred_element_type=jnp.float32
    )


def body(electric, trial, counts):
    capacity = electric.shape[1]
    points = electric.shape[2]
    mode_count = trial.shape[2]
    trial_flat = trial.reshape(points, 2 * mode_count)
    group_index = lax.axis_index("elec")
    live_count = lax.dynamic_slice_in_dim(counts, group_index, 1, 0)[0]
    total_live = jnp.sum(counts.astype(jnp.float32))
    partial_margins = margin_block(electric, trial_flat, mode_count)
    margins = lax.psum(partial_margins, "grid")
    slot_ids = jnp.arange(capacity, dtype=jnp.int32)
    weights = jnp.where(slot_ids < live_count, 1.0, 0.0).astype(jnp.float32) * (
        1.0 / jnp.sqrt(total_live)
    )
    coefs = (margins * weights[None, :, None]).astype(jnp.bfloat16)
    coef_real = coefs[0]
    coef_imag = coefs[1]
    share = points // lax.axis_size("elec")
    mine = lax.psum_scatter(
        field_block(electric, coef_real, coef_imag), "elec", scatter_dimension=0, tiled=True
    )
    return mine.reshape(share, 2, mode_count)


def solution(mesh):
    placed = (P(None, "elec", "grid"), P("grid", None, None), P())
    return jax.shard_map(
        body, mesh=mesh, in_specs=placed, out_specs=P(("grid", "elec"), None, None), check_vma=False
    )
```

profile of v0, /device:TPU:0, one launch (start us, length us, event | category | flops | bytes accessed | tf_op | source)
XLA Modules:
  0.0 126.5 jit_solution(7639683581927419735)
XLA Ops:
  6.5 0.0 all-reduce.2.cloned.1.call-start
  6.5 6.1 %fusion = f32[2048,256]{1,0:T(8,128)S(1)} fusion(bf16[2048,2048]{1,0:T(8,128)(2,1)} %bitcast.22, bf16[256,8,2,128]{3,2,1,0:T(2,128)(2,1)} %bitcast.24), kind=kOutput, calls=%fused_computation.1 | convolution fusion | flops 2147483648 | bytes 11534336 | tf_op jit(solution)/shard_map/dot_general | solution.py:10
  12.6 0.1 fusion.11
  12.7 0.0 copy-start
  12.7 1.1 pad_maximum_fusion
  13.8 0.0 all-reduce.2.cloned.1.call-update
  13.9 0.0 reduce-scatter.2.cloned.1.call-start
  13.9 0.0 copy-done
  13.9 0.6 convert_reduce_fusion
  15.2 0.6 dynamic_slice.3
  15.8 0.6 select_multiply_fusion
  16.5 52.2 %all-reduce.2.cloned.1.call-done = f32[2,1024,128]{2,1,0:T(8,128)} async-done(((f32[2,1024,128]{2,1,0:T(8,128)}), f32[2,1024,128]{2,1,0:T(8,128)}) %all-reduce.2.cloned.1.call-update) | async-done | bytes 1048592 | tf_op jit(solution)/shard_map/psum | solution.py:36
  68.7 1.4 %multiply_convert_fusion = bf16[2,1024,128]{2,1,0:T(8,128)(2,1)S(1)} fusion(f32[2,1024,128]{2,1,0:T(8,128)} %all-reduce.2.cloned.1.call-done, f32[1024]{0:T(1024)S(1)} %select_multiply_fusion), kind=kLoop, calls=%fused_computation.12 | loop fusion | flops 524288 | bytes 1576960 | tf_op jit(solution)/shard_map/convert_element_type | solution.py:41
  70.2 7.1 %convolution_bitcast_fusion = f32[2048,256]{0,1:T(8,128)} fusion(bf16[2048,2048]{1,0:T(8,128)(2,1)} %bitcast.23, bf16[1024,128]{1,0:T(8,128)(2,1)S(1)} %get-tuple-element.8, bf16[1024,128]{1,0:T(8,128)(2,1)S(1)} %fusion.13, bf16[1024,128]{1,0:T(8,128)(2,1)S(1)} %get-tuple-element.7), kind=kOutput, calls=%fused_computation | convolution fusion | flops 2151677952 | bytes 11272192 | tf_op jit(solution)/shard_map/dot_general | solution.py:22
  77.3 0.0 reduce-scatter.2.cloned.1.call-update
  77.3 40.5 %reduce-scatter.2.cloned.1.call-done = f32[256,256]{0,1:T(8,128)} async-done(((f32[2048,256]{0,1:T(8,128)}), f32[256,256]{0,1:T(8,128)}) %reduce-scatter.2.cloned.1.call-update) | async-done | bytes 262160 | tf_op jit(solution)/shard_map/reduce_scatter | solution.py:45
  117.8 1.8 %copy.4 = f32[256,2,128]{2,1,0:T(2,128)} copy(f32[256,2,128]{0,2,1:T(8,128)} %bitcast.21) | data formatting | bytes 524288 | tf_op jit(solution)/shard_map/reshape | solution.py:48
  (2 shorter events, 0.1 us)
Async XLA Ops:
  6.5 62.1 %all-reduce.2.cloned.1.call-start = ((), (), s32[]{:S(2)}) async-start(), calls=%async_computation.1 | async-start | bytes 2097152 | tf_op jit(solution)/shard_map/psum | solution.py:36
  12.7 1.2 copy-start
  13.9 104.0 %reduce-scatter.2.cloned.1.call-start = ((), (), s32[]{:S(2)}) async-start(), calls=%async_computation.2 | async-start | bytes 2359296 | tf_op jit(solution)/shard_map/reduce_scatter | solution.py:45
Sparse Core Ops, SparseCore 0:
  14.0 54.6 all-reduce.1
  77.4 40.3 reduce-scatter.1
where the time goes:
time: 127 us; the launch traced here: 126 us
  waiting for transfers between devices  92.7 us (73%)
  between operations  14.2 us (11%)
  matrix products  13.2 us (10%)
  other arithmetic  3.91 us (3%)
  local copies, waits for them, and re-layouts  2.41 us (2%)
    psum x1, waiting for transfers between devices, body(): margins = lax.psum(partial_margins, 'grid')  52.2 us
    reduce_scatter x1, waiting for transfers between devices, body(): lax.psum_scatter(field_block(electric, coef_real, coef_imag), 'elec', sca...  40.5 us
    dot_general x1, matrix products, field_block(): lax.dot_general(flattened, coef_matrix, (((0,), (0,)), ((), ())), preferr...  7.11 us
    dot_general x1, matrix products, margin_block(): jnp.dot(flattened, trial_flat, preferred_element_type=jnp.float32)  6.08 us
  transfers between devices with their start and end apart: 2, of which 2 were waited for; matrix products, arithmetic and copies ran while one was open for 1% of the time, Pallas kernels for 0%

commit v1 on v0

--- a/solution.py
+++ b/solution.py
@@ -33,7 +33,8 @@
     live_count = lax.dynamic_slice_in_dim(counts, group_index, 1, 0)[0]
     total_live = jnp.sum(counts.astype(jnp.float32))
     partial_margins = margin_block(electric, trial_flat, mode_count)
-    margins = lax.psum(partial_margins, "grid")
+    parts = lax.all_gather(partial_margins, "grid", axis=0, tiled=False)
+    margins = parts.sum(axis=0)
     slot_ids = jnp.arange(capacity, dtype=jnp.int32)
     weights = jnp.where(slot_ids < live_count, 1.0, 0.0).astype(jnp.float32) * (
         1.0 / jnp.sqrt(total_live)

time: 127 us -> 156 us (1.23)
  waiting for transfers between devices: 92.7 us -> 121 us
    all_gather x0 -> x1, waiting for transfers between devices: none -> 81 us  [body(): parts = lax.all_gather(partial_margins, 'grid', axis=0, tiled=False)]
    psum x1 -> x0, waiting for transfers between devices: 52.2 us -> none  [body(): margins = lax.psum(partial_margins, 'grid')]
    reduce_sum x0 -> x1, other arithmetic: none -> 2.56 us  [body(): margins = parts.sum(axis=0)]
where the time goes in v1:
time: 156 us
  waiting for transfers between devices  121 us (78%)
  between operations  14.2 us (9%)
  matrix products  13.2 us (8%)
  other arithmetic  5.19 us (3%)
  local copies, waits for them, and re-layouts  2.41 us (2%)
    all_gather x1, waiting for transfers between devices, body(): parts = lax.all_gather(partial_margins, 'grid', axis=0, tiled=False)  81 us
    reduce_scatter x1, waiting for transfers between devices, body(): lax.psum_scatter(field_block(electric, coef_real, coef_imag), 'elec', sca...  39.8 us
    dot_general x1, matrix products, field_block(): lax.dot_general(flattened, coef_matrix, (((0,), (0,)), ((), ())), preferr...  7.1 us
    dot_general x1, matrix products, margin_block(): jnp.dot(flattened, trial_flat, preferred_element_type=jnp.float32)  6.08 us
  transfers between devices with their start and end apart: 2, of which 2 were waited for; matrix products, arithmetic and copies ran while one was open for 1% of the time, Pallas kernels for 0%

profile of v1, /device:TPU:0, one launch (start us, length us, event | category | flops | bytes accessed | tf_op | source)
XLA Modules:
  0.0 155.8 jit_solution(13078052573977622752)
XLA Ops:
  6.5 0.0 all-gather.3.cloned.1.call-start
  6.5 6.1 %fusion = f32[2048,256]{1,0:T(8,128)S(1)} fusion(bf16[2048,2048]{1,0:T(8,128)(2,1)} %bitcast.24, bf16[256,8,2,128]{3,2,1,0:T(2,128)(2,1)} %bitcast.26), kind=kOutput, calls=%fused_computation.1 | convolution fusion | flops 2147483648 | bytes 11534336 | tf_op jit(solution)/shard_map/dot_general | solution.py:10
  12.6 0.1 fusion.11
  12.7 0.0 copy-start
  12.7 1.0 pad_maximum_fusion
  13.8 0.0 all-gather.3.cloned.1.call-update
  13.8 0.0 reduce-scatter.2.cloned.1.call-start
  13.9 0.0 copy-done
  13.9 0.6 convert_reduce_fusion
  15.2 0.6 dynamic_slice.3
  15.8 0.6 select_multiply_fusion
  16.4 81.0 %all-gather.3.cloned.1.call-done = f32[8,1024,128]{2,1,0:T(8,128)} async-done(((f32[2,1024,128]{2,1,0:T(8,128)}), f32[8,1024,128]{2,1,0:T(8,128)}) %all-gather.3.cloned.1.call-update) | async-done | bytes 4194320 | tf_op jit(solution)/shard_map/all_gather | solution.py:36
  97.5 2.6 %reduce_sum.18 = f32[2,1024,128]{2,1,0:T(8,128)S(1)} reduce(f32[4,2,1024,128]{3,2,1,0:T(8,128)} %bitcast.22, f32[]{:T(128)} %constant.5.clone.1), dimensions={0}, to_apply=%region_0.0 | reduce | flops 786432 | bytes 5242884 | tf_op jit(solution)/shard_map/reduce_sum | solution.py:37
  100.0 0.2 multiply_convert_fusion
  100.3 7.1 %convolution_bitcast_fusion = f32[2048,256]{0,1:T(8,128)} fusion(bf16[2048,2048]{1,0:T(8,128)(2,1)} %bitcast.25, bf16[1024,128]{1,0:T(8,128)(2,1)S(1)} %get-tuple-element.8, bf16[1024,128]{1,0:T(8,128)(2,1)S(1)} %fusion.13, bf16[1024,128]{1,0:T(8,128)(2,1)S(1)} %get-tuple-element.7), kind=kOutput, calls=%fused_computation | convolution fusion | flops 2151677952 | bytes 11272192 | tf_op jit(solution)/shard_map/dot_general | solution.py:22
  107.4 0.0 reduce-scatter.2.cloned.1.call-update
  107.5 39.8 %reduce-scatter.2.cloned.1.call-done = f32[256,256]{0,1:T(8,128)} async-done(((f32[2048,256]{0,1:T(8,128)}), f32[256,256]{0,1:T(8,128)}) %reduce-scatter.2.cloned.1.call-update) | async-done | bytes 262160 | tf_op jit(solution)/shard_map/reduce_scatter | solution.py:46
  147.2 1.8 %copy.5 = f32[256,2,128]{2,1,0:T(2,128)} copy(f32[256,2,128]{0,2,1:T(8,128)} %bitcast.23) | data formatting | bytes 524288 | tf_op jit(solution)/shard_map/reshape | solution.py:49
  (2 shorter events, 0.1 us)
Async XLA Ops:
  6.5 90.9 %all-gather.3.cloned.1.call-start = ((), (), s32[]{:S(2)}) async-start(), calls=%async_computation.2 | async-start | bytes 5242880 | tf_op jit(solution)/shard_map/all_gather | solution.py:36
  12.7 1.1 copy-start
  13.8 133.4 %reduce-scatter.2.cloned.1.call-start = ((), (), s32[]{:S(2)}) async-start(), calls=%async_computation.1 | async-start | bytes 2359296 | tf_op jit(solution)/shard_map/reduce_scatter | solution.py:46
Sparse Core Ops, SparseCore 0:
  13.9 83.4 all-gather.2
  107.6 39.6 reduce-scatter.1
